TPU v7x, 32 devices: a whole 2x2x4 slice. The times are simulated.
32 devices in a mesh: blk: 16 (over z, y, core), tok: 2 (over x).
Axes of the slice: x: 2, y: 2, z: 4, core: 2. Of those that a mesh axis runs over, the one named last changes fastest.
Arguments:
- tokens: bfloat16 [64, 8192], P(('blk', 'tok')), may hold values from -6 to 6
- upstream: bfloat16 [64, 8192], P(('blk', 'tok')), may hold values from -6 to 6
- gate_weight: bfloat16 [14336, 8192], P('blk'), may hold values from -0.0625 to 0.0625
- up_weight: bfloat16 [14336, 8192], P('blk'), may hold values from -0.0625 to 0.0625
- down_weight: bfloat16 [14336, 8192], P('blk'), may hold values from -0.046875 to 0.046875
Outputs:
- mixed: bfloat16 [64, 8192], P(('blk', 'tok'))
- input_grad: bfloat16 [64, 8192], P(('blk', 'tok'))
- gate_weight_grad: bfloat16 [14336, 8192], P('blk', 'tok')
- up_weight_grad: bfloat16 [14336, 8192], P('blk', 'tok')
- down_weight_grad: bfloat16 [14336, 8192], P('blk', 'tok')
All inputs are finite; a program needn't handle non-finite values.
Results may differ from a plain program's by a relative error of at most 0.0049.
Values may be sent and summed in bfloat16 or wider, within the bound.
A program may use at most 192 MiB of HBM per device.

v0:
```python
import jax
import jax.numpy as jnp
from jax import lax
from jax.sharding import PartitionSpec as P


def swapped(block, axis, distance):
    count = lax.axis_size(axis)
    route = []
    for low in range(count):
        high = low | 1 << distance
        if high != low and high < count:
            route += [(low, high), (high, low)]
    return lax.ppermute(block, axis, route)


def right_product(left, right):
    return lax.dot_general(
        left, right, (((1,), (1,)), ((), ())), preferred_element_type=jnp.float32
    )


def left_product(left, right):
    return lax.dot_general(
        left, right, (((0,), (0,)), ((), ())), preferred_element_type=jnp.float32
    )


def rounds(axis):
    count = lax.axis_size(axis)
    levels = count.bit_length() - 1
    assert count == 1 << levels
    return range(levels)


def gathered(block, axis):
    for distance in reversed(rounds(axis)):
        block = jnp.concatenate([block, swapped(block, axis, distance)], axis=0)
    return block


def scattered(term, axis):
    for distance in rounds(axis):
        half = term.shape[0] // 2
        term = term[:half] + swapped(
            term[half:].astype(jnp.bfloat16), axis, distance
        ).astype(jnp.float32)
    return term


def local(tokens, upstream, gate_weight, up_weight, down_weight):
    rows_in = gathered(tokens, "blk")
    grads_in = gathered(upstream, "blk")
    width = rows_in.shape[1]
    half_width = width // 2
    tok_index = lax.axis_index("tok")
    own_start = tok_index * half_width
    other_start = (1 - tok_index) * half_width

    def both_groups(rows):
        own = lax.dynamic_slice_in_dim(rows, own_start, half_width, 1)
        sent = lax.dynamic_slice_in_dim(rows, other_start, half_width, 1)
        return jnp.concatenate([own, swapped(sent, "tok", 0)], axis=0)

    gate_value = right_product(rows_in, gate_weight)
    up_value = right_product(rows_in, up_weight)
    gate_sigmoid = jax.nn.sigmoid(gate_value)
    swish_gate = gate_value * gate_sigmoid
    hidden = (swish_gate * up_value).astype(jnp.bfloat16)
    hidden_grad = right_product(grads_in, down_weight)
    gate_grad = (
        hidden_grad * up_value * gate_sigmoid * (1.0 + gate_value * (1.0 - gate_sigmoid))
    ).astype(jnp.bfloat16)
    up_grad = (hidden_grad * swish_gate).astype(jnp.bfloat16)
    output_term = jnp.dot(hidden, down_weight, preferred_element_type=jnp.float32)
    input_term = jnp.dot(gate_grad, gate_weight, preferred_element_type=jnp.float32) + jnp.dot(
        up_grad, up_weight, preferred_element_type=jnp.float32
    )
    mixed = scattered(output_term, "blk").astype(jnp.bfloat16)
    input_grad = scattered(input_term, "blk").astype(jnp.bfloat16)
    all_rows = both_groups(rows_in)
    all_grads = both_groups(grads_in)
    all_hidden, all_gate, all_up = (
        jnp.concatenate([part, swapped(part, "tok", 0)], axis=0)
        for part in (hidden, gate_grad, up_grad)
    )
    return (
        mixed,
        input_grad,
        left_product(all_gate, all_rows).astype(jnp.bfloat16),
        left_product(all_up, all_rows).astype(jnp.bfloat16),
        left_product(all_hidden, all_grads).astype(jnp.bfloat16),
    )


def solution(mesh):
    return jax.shard_map(
        local,
        mesh=mesh,
        in_specs=(
            P(("blk", "tok"), None),
            P(("blk", "tok"), None),
            P("blk", None),
            P("blk", None),
            P("blk", None),
        ),
        out_specs=(
            P(("blk", "tok"), None),
            P(("blk", "tok"), None),
            P("blk", "tok"),
            P("blk", "tok"),
            P("blk", "tok"),
        ),
        check_vma=False,
    )
```

profile of v0, /device:TPU:0, one launch (start us, length us, event | category | flops | bytes accessed | tf_op | source)
XLA Modules:
  0.0 106.3 jit_solution(434547304285583867)
XLA Ops:
  0.6 4.1 %collective-permute-start = (bf16[2,8192]{1,0:T(2,128)(2,1)}, bf16[2,8192]{1,0:T(2,128)(2,1)S(1)}, u32[]{:S(2)}, u32[]{:S(2)}) collective-permute-start(bf16[2,8192]{1,0:T(2,128)(2,1)} %param.5), channel_id=1, source_target_pairs={{0,16},{16,0},{2,18},{18,2},{4,20},{20,4},{6,22},{22,6},{8,24},{24... | collective-permute-start | bytes 98312 | tf_op jit(solution)/shard_map/ppermute | solution.py:14
  4.8 0.1 collective-permute-start.8
  4.8 2.4 %collective-permute-done = bf16[2,8192]{1,0:T(2,128)(2,1)S(1)} collective-permute-done((bf16[2,8192]{1,0:T(2,128)(2,1)}, bf16[2,8192]{1,0:T(2,128)(2,1)S(1)}, u32[]{:S(2)}, u32[]{:S(2)}) %collective-permute-start) | collective-permute-done | bytes 32800 | tf_op jit(solution)/shard_map/ppermute | solution.py:14
  7.2 0.8 pad_maximum_fusion.7
  8.1 1.8 %collective-permute-start.1 = (bf16[4,8192]{1,0:T(4,128)(2,1)S(1)}, bf16[4,8192]{1,0:T(4,128)(2,1)S(1)}, u32[]{:S(2)}, u32[]{:S(2)}) collective-permute-start(bf16[4,8192]{1,0:T(4,128)(2,1)S(1)} %pad_maximum_fusion.7), channel_id=1, source_target_pairs={{0,8},{8,0},{2,10},{10,2},{4,12},{12,4},{6,14},{14,6},{16,24},{24,... | collective-permute-start | bytes 196616 | tf_op jit(solution)/shard_map/ppermute | solution.py:14
  9.8 0.8 pad_maximum_fusion.8
  10.7 1.6 %collective-permute-start.9 = (bf16[4,8192]{1,0:T(4,128)(2,1)S(1)}, bf16[4,8192]{1,0:T(4,128)(2,1)S(1)}, u32[]{:S(2)}, u32[]{:S(2)}) collective-permute-start(bf16[4,8192]{1,0:T(4,128)(2,1)S(1)} %pad_maximum_fusion.8), channel_id=1, source_target_pairs={{0,8},{8,0},{2,10},{10,2},{4,12},{12,4},{6,14},{14,6},{16,24},{24,... | collective-permute-start | bytes 196616 | tf_op jit(solution)/shard_map/ppermute | solution.py:14
  12.3 0.6 collective-permute-done.1
  12.9 0.9 pad_maximum_fusion.5
  13.8 2.0 %collective-permute-start.2 = (bf16[8,8192]{1,0:T(8,128)(2,1)S(1)}, bf16[8,8192]{1,0:T(8,128)(2,1)S(1)}, u32[]{:S(2)}, u32[]{:S(2)}) collective-permute-start(bf16[8,8192]{1,0:T(8,128)(2,1)S(1)} %pad_maximum_fusion.5), channel_id=1, source_target_pairs={{0,4},{4,0},{2,6},{6,2},{8,12},{12,8},{10,14},{14,10},{16,20},{20,... | collective-permute-start | bytes 393224 | tf_op jit(solution)/shard_map/ppermute | solution.py:14
  15.7 0.9 pad_maximum_fusion.6
  16.6 0.9 collective-permute-start.10
  17.5 2.0 %collective-permute-done.2 = bf16[8,8192]{1,0:T(8,128)(2,1)S(1)} collective-permute-done((bf16[8,8192]{1,0:T(8,128)(2,1)S(1)}, bf16[8,8192]{1,0:T(8,128)(2,1)S(1)}, u32[]{:S(2)}, u32[]{:S(2)}) %collective-permute-start.2) | collective-permute-done | bytes 131104 | tf_op jit(solution)/shard_map/ppermute | solution.py:14
  19.5 0.9 pad_maximum_fusion.3
  20.4 0.1 collective-permute-start.3
  20.5 1.1 %collective-permute-done.10 = bf16[8,8192]{1,0:T(8,128)(2,1)S(1)} collective-permute-done((bf16[8,8192]{1,0:T(8,128)(2,1)S(1)}, bf16[8,8192]{1,0:T(8,128)(2,1)S(1)}, u32[]{:S(2)}, u32[]{:S(2)}) %collective-permute-start.10) | collective-permute-done | bytes 131104 | tf_op jit(solution)/shard_map/ppermute | solution.py:14
  21.6 0.9 pad_maximum_fusion.4
  22.6 0.1 collective-permute-start.11
  22.7 1.0 concatenate.48
  23.7 9.6 %fusion.19 = f32[32,896]{1,0:T(8,128)S(1)} fusion(bf16[32,8192]{1,0:T(8,128)(2,1)S(1)} %concatenate.48, bf16[896,8192]{1,0:T(8,128)(2,1)} %param.8), kind=kOutput, calls=%fused_computation.54 | convolution fusion | flops 469762048 | bytes 15319040 | tf_op jit(solution)/shard_map/dot_general | solution.py:18
  33.3 9.6 %fusion.18 = f32[32,896]{1,0:T(8,128)S(1)} fusion(bf16[32,8192]{1,0:T(8,128)(2,1)S(1)} %concatenate.48, bf16[896,8192]{1,0:T(8,128)(2,1)} %param.7), kind=kOutput, calls=%fused_computation.53 | convolution fusion | flops 469762048 | bytes 15319040 | tf_op jit(solution)/shard_map/dot_general | solution.py:18
  42.9 0.4 concatenate.52
  43.3 9.8 %multiply_convert_fusion = (bf16[32,896]{1,0:T(8,128)(2,1)S(1)}, bf16[32,896]{1,0:T(8,128)(2,1)S(1)}, bf16[32,896]{1,0:T(8,128)(2,1)S(1)}) fusion(f32[32,896]{1,0:T(8,128)S(1)} %fusion.18, f32[32,896]{1,0:T(8,128)S(1)} %fusion.19, bf16[32,8192]{1,0:T(8,128)(2,1)S(1)} %concatenate.52, bf16[896,8192]{1,0:T(8,128)(2,1)} %param.9), kind=kOutput, calls=%fused_computation.33 | convolution fusion | flops 470192128 | bytes 15605760 | tf_op jit(solution)/shard_map/dot_general | solution.py:18
  53.1 1.6 %collective-permute-start.19 = (bf16[32,896]{1,0:T(8,128)(2,1)S(1)}, bf16[32,896]{1,0:T(8,128)(2,1)S(1)}, u32[]{:S(2)}, u32[]{:S(2)}) collective-permute-start(bf16[32,896]{1,0:T(8,128)(2,1)S(1)} %get-tuple-element.11), channel_id=1, source_target_pairs={{0,1},{1,0},{2,3},{3,2},{4,5},{5,4},{6,7},{7,6},{8,9},{9,8},{10,11... | collective-permute-start | bytes 172040 | tf_op jit(solution)/shard_map/ppermute | solution.py:14
  54.7 8.5 %fusion.20 = f32[32,8192]{1,0:T(8,128)S(1)} fusion(bf16[32,896]{1,0:T(8,128)(2,1)S(1)} %get-tuple-element.11, bf16[896,8192]{1,0:T(8,128)(2,1)} %param.9), kind=kOutput, calls=%fused_computation.55 | convolution fusion | flops 469762048 | bytes 15785984 | tf_op jit(solution)/shard_map/dot_general | solution.py:75
  63.2 0.2 collective-permute-start.16
  63.4 2.7 %fusion.21 = f32[32,8192]{1,0:T(8,128)S(1)} fusion(bf16[32,896]{1,0:T(8,128)(2,1)S(1)} %get-tuple-element.10, bf16[896,8192]{1,0:T(8,128)(2,1)S(1)} %bitcast.13), kind=kOutput, calls=%fused_computation.56 | convolution fusion | flops 469762048 | bytes 15785984 | tf_op jit(solution)/shard_map/dot_general | solution.py:76
  66.2 2.0 %collective-permute-start.17 = (bf16[32,4096]{1,0:T(8,128)(2,1)S(1)}, bf16[32,4096]{1,0:T(8,128)(2,1)S(1)}, u32[]{:S(2)}, u32[]{:S(2)}) collective-permute-start(bf16[32,4096]{1,0:T(8,128)(2,1)S(1)} %get-tuple-element.8), channel_id=1, source_target_pairs={{0,1},{1,0},{2,3},{3,2},{4,5},{5,4},{6,7},{7,6},{8,9},{9,8},{10,11... | collective-permute-start | bytes 786440 | tf_op jit(solution)/shard_map/ppermute | solution.py:14
  68.2 0.1 collective-permute-start.18
  68.4 2.7 %convolution_add_fusion = f32[32,8192]{1,0:T(8,128)S(1)} fusion(f32[32,8192]{1,0:T(8,128)S(1)} %fusion.21, bf16[32,896]{1,0:T(8,128)(2,1)S(1)} %get-tuple-element.9, bf16[896,8192]{1,0:T(8,128)(2,1)S(1)} %bitcast.15), kind=kOutput, calls=%fused_computation | convolution fusion | flops 470024192 | bytes 16834560 | tf_op jit(solution)/shard_map/dot_general | solution.py:76
  71.2 0.5 collective-permute-start.12
  71.8 1.1 %collective-permute-done.12 = bf16[16,8192]{1,0:T(8,128)(2,1)S(1)} collective-permute-done((bf16[16,8192]{1,0:T(8,128)(2,1)S(1)}, bf16[16,8192]{1,0:T(8,128)(2,1)S(1)}, u32[]{:S(2)}, u32[]{:S(2)}) %collective-permute-start.12) | collective-permute-done | bytes 262176 | tf_op jit(solution)/shard_map/ppermute | solution.py:14
  72.9 1.9 %collective-permute-start.20 = (bf16[32,4096]{1,0:T(8,128)(2,1)S(1)}, bf16[32,4096]{1,0:T(8,128)(2,1)S(1)}, u32[]{:S(2)}, u32[]{:S(2)}) collective-permute-start(bf16[32,4096]{1,0:T(8,128)(2,1)S(1)} %get-tuple-element.6), channel_id=1, source_target_pairs={{0,1},{1,0},{2,3},{3,2},{4,5},{5,4},{6,7},{7,6},{8,9},{9,8},{10,11... | collective-permute-start | bytes 786440 | tf_op jit(solution)/shard_map/ppermute | solution.py:14
  74.9 0.8 collective-permute-done.18
  75.7 1.0 collective-permute-start.5
  76.7 1.0 collective-permute-start.13
  77.7 5.1 %convolution_convert_fusion.1 = bf16[896,4096]{1,0:T(8,128)(2,1)} fusion(bf16[32,4096]{1,0:T(8,128)(2,1)S(1)} %collective-permute-done.17, bf16[32,4096]{1,0:T(8,128)(2,1)S(1)} %get-tuple-element.7, bf16[32,896]{1,0:T(8,128)(2,1)S(1)} %collective-permute-done.18, bf16[32,896]{1,0:T(8,128)(2,1)S(1)} %get-tuple-element.9), kind=kOutput, calls=%fused_computation.2 | convolution fusion | flops 474710016 | bytes 7979008 | tf_op jit(solution)/shard_map/dot_general | solution.py:24
  82.9 5.4 %convolution_convert_fusion.2 = bf16[896,4096]{1,0:T(8,128)(2,1)} fusion(bf16[32,4096]{1,0:T(8,128)(2,1)S(1)} %collective-permute-done.17, bf16[32,4096]{1,0:T(8,128)(2,1)S(1)} %get-tuple-element.7, bf16[32,896]{1,0:T(8,128)(2,1)S(1)} %collective-permute-done.16, bf16[32,896]{1,0:T(8,128)(2,1)S(1)} %get-tuple-element.10), kind=kOutput, calls=%fused_computation.3 | convolution fusion | flops 474710016 | bytes 7979008 | tf_op jit(solution)/shard_map/dot_general | solution.py:24
  88.3 5.2 %convolution_convert_fusion = bf16[896,4096]{1,0:T(8,128)(2,1)} fusion(bf16[32,4096]{1,0:T(8,128)(2,1)S(1)} %collective-permute-done.20, bf16[32,4096]{1,0:T(8,128)(2,1)S(1)} %get-tuple-element.5, bf16[32,896]{1,0:T(8,128)(2,1)S(1)} %collective-permute-done.19, bf16[32,896]{1,0:T(8,128)(2,1)S(1)} %get-tuple-element.11), kind=kOutput, calls=%fused_computation.1 | convolution fusion | flops 474710016 | bytes 7979008 | tf_op jit(solution)/shard_map/dot_general | solution.py:24
  93.5 1.4 %collective-permute-start.6 = (bf16[4,8192]{1,0:T(4,128)(2,1)S(1)}, bf16[4,8192]{1,0:T(4,128)(2,1)S(1)}, u32[]{:S(2)}, u32[]{:S(2)}) collective-permute-start(bf16[4,8192]{1,0:T(4,128)(2,1)S(1)} %slice.113), channel_id=1, source_target_pairs={{0,8},{8,0},{2,10},{10,2},{4,12},{12,4},{6,14},{14,6},{16,24},{24,... | collective-permute-start | bytes 196616 | tf_op jit(solution)/shard_map/ppermute | solution.py:14
  95.0 0.7 collective-permute-start.14
  95.7 2.1 %collective-permute-done.6 = bf16[4,8192]{1,0:T(4,128)(2,1)S(1)} collective-permute-done((bf16[4,8192]{1,0:T(4,128)(2,1)S(1)}, bf16[4,8192]{1,0:T(4,128)(2,1)S(1)}, u32[]{:S(2)}, u32[]{:S(2)}) %collective-permute-start.6) | collective-permute-done | bytes 65568 | tf_op jit(solution)/shard_map/ppermute | solution.py:14
  97.9 2.8 %collective-permute-start.7 = (bf16[2,8192]{1,0:T(2,128)(2,1)S(1)}, bf16[2,8192]{1,0:T(2,128)(2,1)S(1)}, u32[]{:S(2)}, u32[]{:S(2)}) collective-permute-start(bf16[2,8192]{1,0:T(2,128)(2,1)S(1)} %slice.115), channel_id=1, source_target_pairs={{0,16},{16,0},{2,18},{18,2},{4,20},{20,4},{6,22},{22,6},{8,24},{24... | collective-permute-start | bytes 98312 | tf_op jit(solution)/shard_map/ppermute | solution.py:14
  100.8 1.5 %collective-permute-start.15 = (bf16[2,8192]{1,0:T(2,128)(2,1)S(1)}, bf16[2,8192]{1,0:T(2,128)(2,1)S(1)}, u32[]{:S(2)}, u32[]{:S(2)}) collective-permute-start(bf16[2,8192]{1,0:T(2,128)(2,1)S(1)} %slice.114), channel_id=1, source_target_pairs={{0,16},{16,0},{2,18},{18,2},{4,20},{20,4},{6,22},{22,6},{8,24},{24... | collective-permute-start | bytes 98312 | tf_op jit(solution)/shard_map/ppermute | solution.py:14
  102.2 0.9 collective-permute-done.7
  103.1 0.7 fusion.14
  103.8 1.8 %collective-permute-done.15 = bf16[2,8192]{1,0:T(2,128)(2,1)S(1)} collective-permute-done((bf16[2,8192]{1,0:T(2,128)(2,1)S(1)}, bf16[2,8192]{1,0:T(2,128)(2,1)S(1)}, u32[]{:S(2)}, u32[]{:S(2)}) %collective-permute-start.15) | collective-permute-done | bytes 32800 | tf_op jit(solution)/shard_map/ppermute | solution.py:14
  105.6 0.7 fusion.13
  (49 shorter events, 0.7 us)
Async XLA Ops:
  0.6 6.6 %collective-permute-start = (bf16[2,8192]{1,0:T(2,128)(2,1)}, bf16[2,8192]{1,0:T(2,128)(2,1)S(1)}, u32[]{:S(2)}, u32[]{:S(2)}) collective-permute-start(bf16[2,8192]{1,0:T(2,128)(2,1)} %param.5), channel_id=1, source_target_pairs={{0,16},{16,0},{2,18},{18,2},{4,20},{20,4},{6,22},{22,6},{8,24},{24... | collective-permute-start | bytes 98312 | tf_op jit(solution)/shard_map/ppermute | solution.py:14
  4.8 5.1 %collective-permute-start.8 = (bf16[2,8192]{1,0:T(2,128)(2,1)}, bf16[2,8192]{1,0:T(2,128)(2,1)S(1)}, u32[]{:S(2)}, u32[]{:S(2)}) collective-permute-start(bf16[2,8192]{1,0:T(2,128)(2,1)} %param.6), channel_id=1, source_target_pairs={{0,16},{16,0},{2,18},{18,2},{4,20},{20,4},{6,22},{22,6},{8,24},{24... | collective-permute-start | bytes 98312 | tf_op jit(solution)/shard_map/ppermute | solution.py:14
  8.1 4.8 %collective-permute-start.1 = (bf16[4,8192]{1,0:T(4,128)(2,1)S(1)}, bf16[4,8192]{1,0:T(4,128)(2,1)S(1)}, u32[]{:S(2)}, u32[]{:S(2)}) collective-permute-start(bf16[4,8192]{1,0:T(4,128)(2,1)S(1)} %pad_maximum_fusion.7), channel_id=1, source_target_pairs={{0,8},{8,0},{2,10},{10,2},{4,12},{12,4},{6,14},{14,6},{16,24},{24,... | collective-permute-start | bytes 196616 | tf_op jit(solution)/shard_map/ppermute | solution.py:14
  10.7 5.1 %collective-permute-start.9 = (bf16[4,8192]{1,0:T(4,128)(2,1)S(1)}, bf16[4,8192]{1,0:T(4,128)(2,1)S(1)}, u32[]{:S(2)}, u32[]{:S(2)}) collective-permute-start(bf16[4,8192]{1,0:T(4,128)(2,1)S(1)} %pad_maximum_fusion.8), channel_id=1, source_target_pairs={{0,8},{8,0},{2,10},{10,2},{4,12},{12,4},{6,14},{14,6},{16,24},{24,... | collective-permute-start | bytes 196616 | tf_op jit(solution)/shard_map/ppermute | solution.py:14
  13.8 5.7 %collective-permute-start.2 = (bf16[8,8192]{1,0:T(8,128)(2,1)S(1)}, bf16[8,8192]{1,0:T(8,128)(2,1)S(1)}, u32[]{:S(2)}, u32[]{:S(2)}) collective-permute-start(bf16[8,8192]{1,0:T(8,128)(2,1)S(1)} %pad_maximum_fusion.5), channel_id=1, source_target_pairs={{0,4},{4,0},{2,6},{6,2},{8,12},{12,8},{10,14},{14,10},{16,20},{20,... | collective-permute-start | bytes 393224 | tf_op jit(solution)/shard_map/ppermute | solution.py:14
  16.6 5.0 %collective-permute-start.10 = (bf16[8,8192]{1,0:T(8,128)(2,1)S(1)}, bf16[8,8192]{1,0:T(8,128)(2,1)S(1)}, u32[]{:S(2)}, u32[]{:S(2)}) collective-permute-start(bf16[8,8192]{1,0:T(8,128)(2,1)S(1)} %pad_maximum_fusion.6), channel_id=1, source_target_pairs={{0,4},{4,0},{2,6},{6,2},{8,12},{12,8},{10,14},{14,10},{16,20},{20,... | collective-permute-start | bytes 393224 | tf_op jit(solution)/shard_map/ppermute | solution.py:14
  20.4 2.2 %collective-permute-start.3 = (bf16[16,8192]{1,0:T(8,128)(2,1)S(1)}, bf16[16,8192]{1,0:T(8,128)(2,1)S(1)}, u32[]{:S(2)}, u32[]{:S(2)}) collective-permute-start(bf16[16,8192]{1,0:T(8,128)(2,1)S(1)} %pad_maximum_fusion.3), channel_id=1, source_target_pairs={{0,2},{2,0},{4,6},{6,4},{8,10},{10,8},{12,14},{14,12},{16,18},{18,... | collective-permute-start | bytes 786440 | tf_op jit(solution)/shard_map/ppermute | solution.py:14
  22.6 20.3 %collective-permute-start.11 = (bf16[16,8192]{1,0:T(8,128)(2,1)S(1)}, bf16[16,8192]{1,0:T(8,128)(2,1)S(1)}, u32[]{:S(2)}, u32[]{:S(2)}) collective-permute-start(bf16[16,8192]{1,0:T(8,128)(2,1)S(1)} %pad_maximum_fusion.4), channel_id=1, source_target_pairs={{0,2},{2,0},{4,6},{6,4},{8,10},{10,8},{12,14},{14,12},{16,18},{18,... | collective-permute-start | bytes 786440 | tf_op jit(solution)/shard_map/ppermute | solution.py:14
  23.7 19.2 %copy-start = (bf16[2,8192]{1,0:T(2,128)(2,1)S(1)}, bf16[2,8192]{1,0:T(2,128)(2,1)}, u32[]{:S(2)}) copy-start(bf16[2,8192]{1,0:T(2,128)(2,1)} %param.6) | copy-start | bytes 98308
  43.3 20.1 %slice-start = ((s8[14680064]{0:T(1024)(128)(4,1)}), s8[4194304]{0:T(1024)(128)(4,1)S(1)}, s32[]{:S(2)}) async-start(s8[14680064]{0:T(1024)(128)(4,1)} %bitcast.12), calls=%async_computation | async-start | bytes 8388608
  43.3 20.1 %slice-start.1 = ((s8[14680064]{0:T(1024)(128)(4,1)}), s8[2097152]{0:T(1024)(128)(4,1)S(1)}, s32[]{:S(2)}) async-start(s8[14680064]{0:T(1024)(128)(4,1)} %bitcast.12), calls=%async_computation.1 | async-start | bytes 4194304
  53.1 10.3 %slice-start.2 = ((s8[14680064]{0:T(1024)(128)(4,1)}), s8[4194304]{0:T(1024)(128)(4,1)S(1)}, s32[]{:S(2)}) async-start(s8[14680064]{0:T(1024)(128)(4,1)} %bitcast.12), calls=%async_computation.2 | async-start | bytes 8388608
  53.1 10.3 %slice-start.3 = ((s8[14680064]{0:T(1024)(128)(4,1)}), s8[4194304]{0:T(1024)(128)(4,1)S(1)}, s32[]{:S(2)}) async-start(s8[14680064]{0:T(1024)(128)(4,1)} %bitcast.12), calls=%async_computation.3 | async-start | bytes 8388608
  53.1 35.1 %collective-permute-start.19 = (bf16[32,896]{1,0:T(8,128)(2,1)S(1)}, bf16[32,896]{1,0:T(8,128)(2,1)S(1)}, u32[]{:S(2)}, u32[]{:S(2)}) collective-permute-start(bf16[32,896]{1,0:T(8,128)(2,1)S(1)} %get-tuple-element.11), channel_id=1, source_target_pairs={{0,1},{1,0},{2,3},{3,2},{4,5},{5,4},{6,7},{7,6},{8,9},{9,8},{10,11... | collective-permute-start | bytes 172040 | tf_op jit(solution)/shard_map/ppermute | solution.py:14
  54.7 13.7 %slice-start.4 = ((s8[14680064]{0:T(1024)(128)(4,1)}), s8[4194304]{0:T(1024)(128)(4,1)S(1)}, s32[]{:S(2)}) async-start(s8[14680064]{0:T(1024)(128)(4,1)} %bitcast.14), calls=%async_computation.4 | async-start | bytes 8388608
  54.7 13.7 %slice-start.5 = ((s8[14680064]{0:T(1024)(128)(4,1)}), s8[4194304]{0:T(1024)(128)(4,1)S(1)}, s32[]{:S(2)}) async-start(s8[14680064]{0:T(1024)(128)(4,1)} %bitcast.14), calls=%async_computation.5 | async-start | bytes 8388608
  63.2 5.2 %slice-start.6 = ((s8[14680064]{0:T(1024)(128)(4,1)}), s8[4194304]{0:T(1024)(128)(4,1)S(1)}, s32[]{:S(2)}) async-start(s8[14680064]{0:T(1024)(128)(4,1)} %bitcast.14), calls=%async_computation.6 | async-start | bytes 8388608
  63.2 5.2 %slice-start.7 = ((s8[14680064]{0:T(1024)(128)(4,1)}), s8[2097152]{0:T(1024)(128)(4,1)S(1)}, s32[]{:S(2)}) async-start(s8[14680064]{0:T(1024)(128)(4,1)} %bitcast.14), calls=%async_computation.7 | async-start | bytes 4194304
  63.2 19.7 %collective-permute-start.16 = (bf16[32,896]{1,0:T(8,128)(2,1)S(1)}, bf16[32,896]{1,0:T(8,128)(2,1)S(1)}, u32[]{:S(2)}, u32[]{:S(2)}) collective-permute-start(bf16[32,896]{1,0:T(8,128)(2,1)S(1)} %get-tuple-element.10), channel_id=1, source_target_pairs={{0,1},{1,0},{2,3},{3,2},{4,5},{5,4},{6,7},{7,6},{8,9},{9,8},{10,11... | collective-permute-start | bytes 172040 | tf_op jit(solution)/shard_map/ppermute | solution.py:14
  66.2 10.5 %collective-permute-start.17 = (bf16[32,4096]{1,0:T(8,128)(2,1)S(1)}, bf16[32,4096]{1,0:T(8,128)(2,1)S(1)}, u32[]{:S(2)}, u32[]{:S(2)}) collective-permute-start(bf16[32,4096]{1,0:T(8,128)(2,1)S(1)} %get-tuple-element.8), channel_id=1, source_target_pairs={{0,1},{1,0},{2,3},{3,2},{4,5},{5,4},{6,7},{7,6},{8,9},{9,8},{10,11... | collective-permute-start | bytes 786440 | tf_op jit(solution)/shard_map/ppermute | solution.py:14
  68.2 7.5 %collective-permute-start.18 = (bf16[32,896]{1,0:T(8,128)(2,1)S(1)}, bf16[32,896]{1,0:T(8,128)(2,1)S(1)}, u32[]{:S(2)}, u32[]{:S(2)}) collective-permute-start(bf16[32,896]{1,0:T(8,128)(2,1)S(1)} %get-tuple-element.9), channel_id=1, source_target_pairs={{0,1},{1,0},{2,3},{3,2},{4,5},{5,4},{6,7},{7,6},{8,9},{9,8},{10,11... | collective-permute-start | bytes 172040 | tf_op jit(solution)/shard_map/ppermute | solution.py:14
  68.3 2.9 %collective-permute-start.4 = (bf16[16,8192]{1,0:T(8,128)(2,1)S(1)}, bf16[16,8192]{1,0:T(8,128)(2,1)S(1)}, u32[]{:S(2)}, u32[]{:S(2)}) collective-permute-start(bf16[16,8192]{1,0:T(8,128)(2,1)S(1)} %slice.109), channel_id=1, source_target_pairs={{0,2},{2,0},{4,6},{6,4},{8,10},{10,8},{12,14},{14,12},{16,18},{18,... | collective-permute-start | bytes 786440 | tf_op jit(solution)/shard_map/ppermute | solution.py:14
  71.2 1.7 %collective-permute-start.12 = (bf16[16,8192]{1,0:T(8,128)(2,1)S(1)}, bf16[16,8192]{1,0:T(8,128)(2,1)S(1)}, u32[]{:S(2)}, u32[]{:S(2)}) collective-permute-start(bf16[16,8192]{1,0:T(8,128)(2,1)S(1)} %slice.108), channel_id=1, source_target_pairs={{0,2},{2,0},{4,6},{6,4},{8,10},{10,8},{12,14},{14,12},{16,18},{18,... | collective-permute-start | bytes 786440 | tf_op jit(solution)/shard_map/ppermute | solution.py:14
  72.9 15.3 %collective-permute-start.20 = (bf16[32,4096]{1,0:T(8,128)(2,1)S(1)}, bf16[32,4096]{1,0:T(8,128)(2,1)S(1)}, u32[]{:S(2)}, u32[]{:S(2)}) collective-permute-start(bf16[32,4096]{1,0:T(8,128)(2,1)S(1)} %get-tuple-element.6), channel_id=1, source_target_pairs={{0,1},{1,0},{2,3},{3,2},{4,5},{5,4},{6,7},{7,6},{8,9},{9,8},{10,11... | collective-permute-start | bytes 786440 | tf_op jit(solution)/shard_map/ppermute | solution.py:14
  75.7 17.7 %collective-permute-start.5 = (bf16[8,8192]{1,0:T(8,128)(2,1)S(1)}, bf16[8,8192]{1,0:T(8,128)(2,1)S(1)}, u32[]{:S(2)}, u32[]{:S(2)}) collective-permute-start(bf16[8,8192]{1,0:T(8,128)(2,1)S(1)} %slice.111), channel_id=1, source_target_pairs={{0,4},{4,0},{2,6},{6,2},{8,12},{12,8},{10,14},{14,10},{16,20},{20,... | collective-permute-start | bytes 393224 | tf_op jit(solution)/shard_map/ppermute | solution.py:14
  76.7 18.2 %collective-permute-start.13 = (bf16[8,8192]{1,0:T(8,128)(2,1)S(1)}, bf16[8,8192]{1,0:T(8,128)(2,1)S(1)}, u32[]{:S(2)}, u32[]{:S(2)}) collective-permute-start(bf16[8,8192]{1,0:T(8,128)(2,1)S(1)} %slice.110), channel_id=1, source_target_pairs={{0,4},{4,0},{2,6},{6,2},{8,12},{12,8},{10,14},{14,10},{16,20},{20,... | collective-permute-start | bytes 393224 | tf_op jit(solution)/shard_map/ppermute | solution.py:14
  93.5 4.3 %collective-permute-start.6 = (bf16[4,8192]{1,0:T(4,128)(2,1)S(1)}, bf16[4,8192]{1,0:T(4,128)(2,1)S(1)}, u32[]{:S(2)}, u32[]{:S(2)}) collective-permute-start(bf16[4,8192]{1,0:T(4,128)(2,1)S(1)} %slice.113), channel_id=1, source_target_pairs={{0,8},{8,0},{2,10},{10,2},{4,12},{12,4},{6,14},{14,6},{16,24},{24,... | collective-permute-start | bytes 196616 | tf_op jit(solution)/shard_map/ppermute | solution.py:14
  95.0 5.7 %collective-permute-start.14 = (bf16[4,8192]{1,0:T(4,128)(2,1)S(1)}, bf16[4,8192]{1,0:T(4,128)(2,1)S(1)}, u32[]{:S(2)}, u32[]{:S(2)}) collective-permute-start(bf16[4,8192]{1,0:T(4,128)(2,1)S(1)} %slice.112), channel_id=1, source_target_pairs={{0,8},{8,0},{2,10},{10,2},{4,12},{12,4},{6,14},{14,6},{16,24},{24,... | collective-permute-start | bytes 196616 | tf_op jit(solution)/shard_map/ppermute | solution.py:14
  97.9 5.2 %collective-permute-start.7 = (bf16[2,8192]{1,0:T(2,128)(2,1)S(1)}, bf16[2,8192]{1,0:T(2,128)(2,1)S(1)}, u32[]{:S(2)}, u32[]{:S(2)}) collective-permute-start(bf16[2,8192]{1,0:T(2,128)(2,1)S(1)} %slice.115), channel_id=1, source_target_pairs={{0,16},{16,0},{2,18},{18,2},{4,20},{20,4},{6,22},{22,6},{8,24},{24... | collective-permute-start | bytes 98312 | tf_op jit(solution)/shard_map/ppermute | solution.py:14
  100.8 4.9 %collective-permute-start.15 = (bf16[2,8192]{1,0:T(2,128)(2,1)S(1)}, bf16[2,8192]{1,0:T(2,128)(2,1)S(1)}, u32[]{:S(2)}, u32[]{:S(2)}) collective-permute-start(bf16[2,8192]{1,0:T(2,128)(2,1)S(1)} %slice.114), channel_id=1, source_target_pairs={{0,16},{16,0},{2,18},{18,2},{4,20},{20,4},{6,22},{22,6},{8,24},{24... | collective-permute-start | bytes 98312 | tf_op jit(solution)/shard_map/ppermute | solution.py:14
where the time goes:
time: 107 us; the launch traced here: 106 us
  matrix products  58.5 us (55%)
  starting transfers between devices  25.3 us (24%)
  waiting for transfers between devices  13 us (12%)
  other arithmetic  6.77 us (6%)
  local copies, waits for them, and re-layouts  1.79 us (2%)
    dot_general x3, matrix products, right_product(): lax.dot_general(left, right, (((1,), (1,)), ((), ())), preferred_element_...  29 us
    ppermute x21, starting transfers between devices, swapped(): return lax.ppermute(block, axis, route)  25.3 us
    dot_general x3, matrix products, left_product(): lax.dot_general(left, right, (((0,), (0,)), ((), ())), preferred_element_...  15.7 us
    ppermute x21, waiting for transfers between devices, swapped(): return lax.ppermute(block, axis, route)  13 us
    dot_general x1, matrix products, local(): jnp.dot(hidden, down_weight, preferred_element_type=jnp.float32)  8.51 us
    concatenate x6, other arithmetic, gathered(): block = jnp.concatenate([block, swapped(block, axis, distance)], axis=0)  5.26 us
    dot_general x1, matrix products, local(): jnp.dot(gate_grad, gate_weight, preferred_element_type=jnp.float32)  2.69 us
    dot_general x1, matrix products, local(): jnp.dot(up_grad, up_weight, preferred_element_type=jnp.float32)  2.69 us
  transfers between devices with their start and end apart: 21, of which 9 were waited for; matrix products, arithmetic and copies ran while one was open for 53% of the time, Pallas kernels for 0%

commit v1 on v0

v1 whole, which is shorter than its diff:
```python
import functools

import jax
import jax.numpy as jnp
from jax import lax
from jax.experimental import pallas as pl
from jax.experimental.pallas import tpu as pltpu
from jax.sharding import PartitionSpec as P

MESH = pl.DeviceIdType.MESH
VMEM_LIMIT = 63 * 1024 * 1024
GATHER_CHUNKS = 4
REDUCE_CHUNKS = 8
GRAD_CHUNKS = 4
GRAD_SLOTS = 3


def drain(ref, sem):
    pltpu.make_async_copy(ref, ref, sem).wait()


def columns(index, width):
    return pl.ds(pl.multiple_of(index * width, width), width)


def right_product(left, right):
    return lax.dot_general(
        left, right, (((1,), (1,)), ((), ())), preferred_element_type=jnp.float32
    )


def block_kernel(
    tokens,
    upstream,
    gate_hbm,
    up_hbm,
    down_hbm,
    mixed,
    input_grad,
    rows_out,
    hidden_out,
    weights,
    rows,
    values,
    hidden,
    own_term,
    pair_send,
    pair_recv,
    sum_send,
    sum_recv,
    weight_sem,
    send_sem,
    recv_sem,
    relay_send_sem,
    relay_recv_sem,
    half_sems,
    hidden_sems,
    pair_send_sem,
    pair_recv_sem,
    sum_send_sem,
    sum_recv_sem,
):
    count = lax.axis_size("blk")
    line = count // 2
    me = lax.axis_index("blk")
    tok = lax.axis_index("tok")
    place = me // 2
    core = me % 2
    sibling = (me + 1 - 2 * core, tok)
    across = (me, 1 - tok)
    own_rows, width = tokens.shape
    half_rows = line * own_rows
    group = 2 * half_rows
    half_width = width // 2
    gather_width = width // GATHER_CHUNKS
    reduce_width = width // REDUCE_CHUNKS
    inputs = (tokens, upstream)

    def peer(step):
        return ((place + step) % line * 2 + core, tok)

    def slot(index):
        return pl.ds(index * own_rows, own_rows)

    for part in range(GATHER_CHUNKS):
        cols = pl.ds(part * gather_width, gather_width)
        for index, hbm in enumerate((gate_hbm, up_hbm, down_hbm)):
            pltpu.make_async_copy(
                hbm.at[:, cols], weights.at[index, :, cols], weight_sem.at[index, part]
            ).start()
        for index, source in enumerate(inputs):
            pltpu.make_async_copy(
                source.at[:, cols], rows.at[index, slot(place), cols], recv_sem.at[index, part]
            ).start()

    barrier = pltpu.get_barrier_semaphore()

    def greet(step, carry):
        pl.semaphore_signal(barrier, inc=1, device_id=peer(step), device_id_type=MESH)
        return carry

    lax.fori_loop(1, line, greet, 0)
    pl.semaphore_signal(barrier, inc=1, device_id=sibling, device_id_type=MESH)
    pl.semaphore_signal(barrier, inc=1, device_id=across, device_id_type=MESH)
    pl.semaphore_wait(barrier, line + 1)

    for part in range(GATHER_CHUNKS):
        cols = pl.ds(part * gather_width, gather_width)

        def spread(step, carry):
            for index, source in enumerate(inputs):
                pltpu.make_async_remote_copy(
                    src_ref=source.at[:, cols],
                    dst_ref=rows.at[index, slot(place), cols],
                    send_sem=send_sem.at[index, step],
                    recv_sem=recv_sem.at[index, part],
                    device_id=peer(step),
                    device_id_type=MESH,
                ).start()
            return carry

        lax.fori_loop(1, line, spread, 0)

    def relay_copy(part, index):
        cols = pl.ds(part * gather_width, gather_width)
        return pltpu.make_async_remote_copy(
            src_ref=rows.at[index, pl.ds(0, half_rows), cols],
            dst_ref=rows.at[index, pl.ds(half_rows, half_rows), cols],
            send_sem=relay_send_sem.at[index, part],
            recv_sem=relay_recv_sem.at[index, part],
            device_id=sibling,
            device_id_type=MESH,
        )

    def relay(part):
        cols = pl.ds(part * gather_width, gather_width)
        for index in range(2):
            drain(rows.at[index, pl.ds(0, half_rows), cols], recv_sem.at[index, part])
            relay_copy(part, index).start()

    other_half = columns(1 - tok, half_width)
    own_half = columns(tok, half_width)
    half_local = [
        pltpu.make_async_copy(
            rows.at[index, :, own_half], rows_out.at[index, pl.ds(0, group)], half_sems.at[index, 0]
        )
        for index in range(2)
    ]
    half_remote = [
        pltpu.make_async_remote_copy(
            src_ref=rows.at[index, :, other_half],
            dst_ref=rows_out.at[index, pl.ds(group, group)],
            send_sem=half_sems.at[index, 1],
            recv_sem=half_sems.at[index, 2],
            device_id=across,
            device_id_type=MESH,
        )
        for index in range(2)
    ]

    relay(0)
    for part in range(GATHER_CHUNKS):
        cols = pl.ds(part * gather_width, gather_width)
        for index, hbm in enumerate((gate_hbm, up_hbm, down_hbm)):
            source = index // 2
            if index != 1:
                relay_copy(part, source).wait_recv()
            if part == GATHER_CHUNKS - 1 and index == 2:
                for copy in half_local + half_remote:
                    copy.start()
            pltpu.make_async_copy(
                hbm.at[:, cols], weights.at[index, :, cols], weight_sem.at[index, part]
            ).wait()
            term = right_product(rows[source, :, cols], weights[index, :, cols])
            if part == 0:
                values[index] = term
            else:
                values[index] += term
            if index == 0 and part + 1 < GATHER_CHUNKS:
                relay(part + 1)

    gate_value = values[0]
    up_value = values[1]
    hidden_grad = values[2]
    gate_sigmoid = jax.nn.sigmoid(gate_value)
    swish_gate = gate_value * gate_sigmoid
    hidden[0] = (
        hidden_grad * up_value * gate_sigmoid * (1.0 + gate_value * (1.0 - gate_sigmoid))
    ).astype(jnp.bfloat16)
    hidden[1] = (hidden_grad * swish_gate).astype(jnp.bfloat16)
    hidden[2] = (swish_gate * up_value).astype(jnp.bfloat16)
    hidden_local = [
        pltpu.make_async_copy(
            hidden.at[index], hidden_out.at[index, pl.ds(0, group)], hidden_sems.at[index, 0]
        )
        for index in range(3)
    ]
    hidden_remote = [
        pltpu.make_async_remote_copy(
            src_ref=hidden.at[index],
            dst_ref=hidden_out.at[index, pl.ds(group, group)],
            send_sem=hidden_sems.at[index, 1],
            recv_sem=hidden_sems.at[index, 2],
            device_id=across,
            device_id_type=MESH,
        )
        for index in range(3)
    ]
    for copy in hidden_local + hidden_remote:
        copy.start()

    def pair_copy(part, index):
        cols = columns(part, reduce_width)
        return pltpu.make_async_remote_copy(
            src_ref=pair_send.at[index, :, cols],
            dst_ref=pair_recv.at[index, :, cols],
            send_sem=pair_send_sem.at[index, part],
            recv_sem=pair_recv_sem.at[index, part],
            device_id=sibling,
            device_id_type=MESH,
        )

    def produce(part):
        cols = columns(part, reduce_width)
        term = jnp.dot(hidden[2], weights[2, :, cols], preferred_element_type=jnp.float32)
        own_term[0, :, cols] = term[:half_rows]
        pair_send[0, :, cols] = term[half_rows:].astype(jnp.bfloat16)
        pair_copy(part, 0).start()
        term = jnp.dot(hidden[0], weights[0, :, cols], preferred_element_type=jnp.float32)
        term += jnp.dot(hidden[1], weights[1, :, cols], preferred_element_type=jnp.float32)
        own_term[1, :, cols] = term[:half_rows]
        pair_send[1, :, cols] = term[half_rows:].astype(jnp.bfloat16)
        pair_copy(part, 1).start()

    def deliver(part):
        cols = columns(part, reduce_width)
        for index in range(2):
            pair_copy(part, index).wait_recv()
            sum_send[index, :, cols] = (
                own_term[index, :, cols] + pair_recv[index, :, cols].astype(jnp.float32)
            ).astype(jnp.bfloat16)
            pltpu.make_async_copy(
                sum_send.at[index, slot(place), cols],
                sum_recv.at[index, slot(place), cols],
                sum_recv_sem.at[index],
            ).start()

            def hand(step, carry):
                pltpu.make_async_remote_copy(
                    src_ref=sum_send.at[index, slot((place + step) % line), cols],
                    dst_ref=sum_recv.at[index, slot(place), cols],
                    send_sem=sum_send_sem.at[index, step],
                    recv_sem=sum_recv_sem.at[index],
                    device_id=peer(step),
                    device_id_type=MESH,
                ).start()
                return carry

            lax.fori_loop(1, line, hand, 0)

    produce(0)

    def advance(part, carry):
        produce(part)
        deliver(part - 1)
        return carry

    lax.fori_loop(1, REDUCE_CHUNKS, advance, 0)
    deliver(REDUCE_CHUNKS - 1)

    for index in range(2):
        drain(sum_recv.at[index], sum_recv_sem.at[index])
    pick = (
        lax.broadcasted_iota(jnp.int32, (own_rows, half_rows), 1) % own_rows
        == lax.broadcasted_iota(jnp.int32, (own_rows, half_rows), 0)
    ).astype(jnp.bfloat16)
    for index, result in enumerate((mixed, input_grad)):
        result[...] = jnp.dot(pick, sum_recv[index], preferred_element_type=jnp.float32).astype(
            jnp.bfloat16
        )

    for index in range(2):

        def sent(step, carry):
            drain(inputs[index], send_sem.at[index, step])
            drain(inputs[index], sum_send_sem.at[index, step])
            return carry

        lax.fori_loop(1, line, sent, 0)
        for part in range(GATHER_CHUNKS):
            relay_copy(part, index).wait_send()
        for part in range(REDUCE_CHUNKS):
            pair_copy(part, index).wait_send()
    for copy in half_local + half_remote + hidden_local + hidden_remote:
        copy.wait()


def block(tokens, upstream, gate_weight, up_weight, down_weight):
    own_rows, width = tokens.shape
    units = gate_weight.shape[0]
    count = lax.axis_size("blk")
    assert count % 2 == 0 and lax.axis_size("tok") == 2
    half_rows = count // 2 * own_rows
    group = 2 * half_rows
    bf16, f32 = jnp.bfloat16, jnp.float32
    hbm = pl.BlockSpec(memory_space=pl.ANY)
    vmem = pl.BlockSpec(memory_space=pltpu.VMEM)
    dma = pltpu.SemaphoreType.DMA
    return pl.pallas_call(
        block_kernel,
        out_shape=(
            jax.ShapeDtypeStruct((own_rows, width), bf16),
            jax.ShapeDtypeStruct((own_rows, width), bf16),
            jax.ShapeDtypeStruct((2, 2 * group, width // 2), bf16),
            jax.ShapeDtypeStruct((3, 2 * group, units), bf16),
        ),
        in_specs=[hbm] * 5,
        out_specs=(vmem, vmem, hbm, hbm),
        scratch_shapes=[
            pltpu.VMEM((3, units, width), bf16),
            pltpu.VMEM((2, group, width), bf16),
            pltpu.VMEM((3, group, units), f32),
            pltpu.VMEM((3, group, units), bf16),
            pltpu.VMEM((2, half_rows, width), f32),
            pltpu.VMEM((2, half_rows, width), bf16),
            pltpu.VMEM((2, half_rows, width), bf16),
            pltpu.VMEM((2, half_rows, width), bf16),
            pltpu.VMEM((2, half_rows, width), bf16),
            dma((3, GATHER_CHUNKS)),
            dma((2, count // 2)),
            dma((2, GATHER_CHUNKS)),
            dma((2, GATHER_CHUNKS)),
            dma((2, GATHER_CHUNKS)),
            dma((2, 3)),
            dma((3, 3)),
            dma((2, REDUCE_CHUNKS)),
            dma((2, REDUCE_CHUNKS)),
            dma((2, count // 2)),
            dma((2,)),
        ],
        compiler_params=pltpu.CompilerParams(
            collective_id=0, has_side_effects=True, vmem_limit_bytes=VMEM_LIMIT
        ),
    )(tokens, upstream, gate_weight, up_weight, down_weight)


def grad_kernel(rows, hidden, gate_grad, up_grad, down_grad, tiles, sems):
    width = rows.shape[2] // GRAD_CHUNKS
    pending = [None] * GRAD_SLOTS
    step = 0
    for index, result in enumerate((gate_grad, up_grad, down_grad)):
        for part in range(GRAD_CHUNKS):
            cols = pl.ds(part * width, width)
            where = step % GRAD_SLOTS
            if pending[where] is not None:
                pending[where].wait()
            tiles[where] = lax.dot_general(
                hidden[index],
                rows[index // 2, :, cols],
                (((0,), (0,)), ((), ())),
                preferred_element_type=jnp.float32,
            ).astype(jnp.bfloat16)
            pending[where] = pltpu.make_async_copy(
                tiles.at[where], result.at[:, cols], sems.at[where]
            )
            pending[where].start()
            step += 1
    for copy in pending:
        if copy is not None:
            copy.wait()


def weight_grads(rows, hidden):
    units = hidden.shape[2]
    width = rows.shape[2]
    hbm = pl.BlockSpec(memory_space=pl.ANY)
    vmem = pl.BlockSpec(memory_space=pltpu.VMEM)
    shape = jax.ShapeDtypeStruct((units, width), jnp.bfloat16)
    return pl.pallas_call(
        grad_kernel,
        out_shape=(shape, shape, shape),
        in_specs=[vmem, vmem],
        out_specs=(hbm, hbm, hbm),
        scratch_shapes=[
            pltpu.VMEM((GRAD_SLOTS, units, width // GRAD_CHUNKS), jnp.bfloat16),
            pltpu.SemaphoreType.DMA((GRAD_SLOTS,)),
        ],
        compiler_params=pltpu.CompilerParams(vmem_limit_bytes=VMEM_LIMIT),
    )(rows, hidden)


def local(*args):
    mixed, input_grad, rows, hidden = block(*args)
    return (mixed, input_grad, *weight_grads(rows, hidden))


def solution(mesh):
    return jax.shard_map(
        local,
        mesh=mesh,
        in_specs=(
            P(("blk", "tok"), None),
            P(("blk", "tok"), None),
            P("blk", None),
            P("blk", None),
            P("blk", None),
        ),
        out_specs=(
            P(("blk", "tok"), None),
            P(("blk", "tok"), None),
            P("blk", "tok"),
            P("blk", "tok"),
            P("blk", "tok"),
        ),
        check_vma=False,
    )
```

time: 107 us -> 63.7 us (0.60)
  Pallas kernels: 0 us -> 60 us
  matrix products: 58.5 us -> 0 us
  starting transfers between devices: 25.3 us -> 0 us
  waiting for transfers between devices: 13 us -> 0 us
  other arithmetic: 6.77 us -> 0 us
    pallas_call x0 -> x2, Pallas kernels: none -> 60 us  [the longest x1 49.6 us: block(): pl.pallas_call(block_kernel, out_shape=(jax.ShapeDtypeStruct((own_rows, w...]
    dot_general x9 -> x0, matrix products: 58.5 us -> none  [the longest x3 29 us: right_product(): lax.dot_general(left, right, (((1,), (1,)), ((), ())), preferred_element_...]
    ppermute x21 -> x0, starting transfers between devices: 25.3 us -> none  [swapped(): return lax.ppermute(block, axis, route)]
    ppermute x21 -> x0, waiting for transfers between devices: 13 us -> none  [swapped(): return lax.ppermute(block, axis, route)]
    concatenate x6 -> x0, other arithmetic: 5.26 us -> none  [gathered(): block = jnp.concatenate([block, swapped(block, axis, distance)], axis=0)]
    unnamed x18 -> x2, local copies, waits for them, and re-layouts: 0.06 us -> 2.79 us
    concatenate x2 -> x0, local copies, waits for them, and re-layouts: 1.4 us -> none  [gathered(): block = jnp.concatenate([block, swapped(block, axis, distance)], axis=0)]
    convert_element_type x2 -> x0, other arithmetic: 1.3 us -> none  [the longest x1 0.65 us: local(): mixed = scattered(output_term, 'blk').astype(jnp.bfloat16)]
  transfers between devices with their start and end apart: 21 -> 0, of which waited for: 9 -> 0; matrix products, arithmetic and copies ran while one was open for 53% -> 0% of each run, Pallas kernels for 0% -> 0%
where the time goes in v1:
time: 63.7 us; the launch traced here: 63.4 us
  Pallas kernels  60 us (94%)
  local copies, waits for them, and re-layouts  2.79 us (4%)
  between operations  0.65 us (1%)
    pallas_call x1, Pallas kernels, block(): pl.pallas_call(block_kernel, out_shape=(jax.ShapeDtypeStruct((own_rows, w...  49.6 us
    pallas_call x1, Pallas kernels, weight_grads(): pl.pallas_call(grad_kernel, out_shape=(shape, shape, shape), in_specs=[vm...  10.4 us
    unnamed x2, local copies, waits for them, and re-layouts  2.79 us

profile of v1, /device:TPU:0, one launch (start us, length us, event | category | flops | bytes accessed | tf_op | source)
XLA Modules:
  0.0 63.4 jit_solution(5393004650263960617)
XLA Ops:
  0.6 49.6 %shard_map.92 = (bf16[2,8192]{1,0:T(2,128)(2,1)}, bf16[2,8192]{1,0:T(2,128)(2,1)}, bf16[2,64,4096]{2,1,0:T(8,128)(2,1)}, bf16[3,64,896]{2,1,0:T(8,128)(2,1)}) custom-call(bf16[2,8192]{1,0:T(2,128)(2,1)} %tokens.1, bf16[2,8192]{1,0:T(2,128)(2,1)} %upstream.1, bf16[896,8192]{1,0:T(8,128)(2,1)} %gate_hbm.1, bf16[896,8192]{1,0:T(8,128)(2,1)} %up_hbm.1, ...), custom_call_target="tpu_custom_call" | custom-call | tf_op jit(solution)/shard_map/pallas_call | solution.py:309
  50.3 10.4 %shard_map.93 = (bf16[896,4096]{1,0:T(8,128)(2,1)}, bf16[896,4096]{1,0:T(8,128)(2,1)}, bf16[896,4096]{1,0:T(8,128)(2,1)}) custom-call(bf16[2,64,4096]{2,1,0:T(8,128)(2,1)} %get-tuple-element.14.rows, bf16[3,64,896]{2,1,0:T(8,128)(2,1)} %get-tuple-element.15.hidden), custom_call_target="tpu_custom_call" | custom-call | tf_op jit(solution)/shard_map/pallas_call | solution.py:379
  60.6 1.4 %copy.12 = bf16[2,8192]{1,0:T(2,128)(2,1)} copy(bf16[2,8192]{1,0:T(2,128)(2,1)} %get-tuple-element.24) | data formatting | bytes 65536
  62.0 1.4 %copy.13 = bf16[2,8192]{1,0:T(2,128)(2,1)} copy(bf16[2,8192]{1,0:T(2,128)(2,1)} %get-tuple-element.25) | data formatting | bytes 65536

commit v2 on v1

v2 whole, which is shorter than its diff:
```python
import functools

import jax
import jax.numpy as jnp
from jax import lax
from jax.experimental import pallas as pl
from jax.experimental.pallas import tpu as pltpu
from jax.sharding import PartitionSpec as P

MESH = pl.DeviceIdType.MESH
VMEM_LIMIT = 63 * 1024 * 1024
GATHER_PARTS = (1, 1, 2, 2, 2)
REDUCE_PARTS = (2, 2, 2, 1, 1)
FOLD_PAIR_LAG = 1
FOLD_SIDE_LAG = 3
GRAD_CHUNKS = 4
GRAD_SLOTS = 3


def drain(ref, sem):
    pltpu.make_async_copy(ref, ref, sem).wait()


def columns(index, width):
    return pl.ds(pl.multiple_of(index * width, width), width)


def pieces(width, shares):
    unit = width // sum(shares)
    starts = [sum(shares[:index]) for index in range(len(shares))]
    return [pl.ds(start * unit, share * unit) for start, share in zip(starts, shares)]


def right_product(left, right):
    return lax.dot_general(
        left, right, (((1,), (1,)), ((), ())), preferred_element_type=jnp.float32
    )


def block_kernel(
    tokens,
    upstream,
    gate_hbm,
    up_hbm,
    down_hbm,
    rows_out,
    hidden_out,
    sums_out,
    weights,
    rows,
    values,
    hidden,
    far_rows,
    own_term,
    pair_send,
    pair_recv,
    side_send,
    side_recv,
    line_send,
    weight_sem,
    send_sem,
    recv_sem,
    side_sems,
    pair_sems,
    far_sems,
    hidden_sems,
    term_pair_sems,
    term_side_sems,
    sum_send_sem,
    sum_recv_sem,
):
    line = lax.axis_size("blk") // 4
    me = lax.axis_index("blk")
    tok = lax.axis_index("tok")
    core = me % 2
    side = me // 2 % 2
    place = me // 4
    sibling = (me + 1 - 2 * core, tok)
    beside = (me + 2 - 4 * side, tok)
    across = (me, 1 - tok)
    own_rows, width = tokens.shape
    quarter = line * own_rows
    half = 2 * quarter
    group = 2 * half
    half_width = width // 2
    inputs = (tokens, upstream)
    gather_cols = pieces(width, GATHER_PARTS)
    reduce_cols = pieces(width, REDUCE_PARTS)
    sources = (gate_hbm, up_hbm, down_hbm)

    def peer(step):
        return ((place + step) % line * 4 + side * 2 + core, tok)

    def slot(index):
        return pl.ds(index * own_rows, own_rows)

    def remote(source, target, sems, where, device):
        return pltpu.make_async_remote_copy(
            src_ref=source,
            dst_ref=target,
            send_sem=sems.at[(0, *where)],
            recv_sem=sems.at[(1, *where)],
            device_id=device,
            device_id_type=MESH,
        )

    def weight_copy(index, part):
        cols = gather_cols[part]
        return pltpu.make_async_copy(
            sources[index].at[:, cols], weights.at[index, :, cols], weight_sem.at[index, part]
        )

    parts = range(len(gather_cols))
    for part in parts:
        for index, source in enumerate(inputs):
            cols = gather_cols[part]
            pltpu.make_async_copy(
                source.at[:, cols], rows.at[index, slot(place), cols], recv_sem.at[index, part]
            ).start()
    for part in parts:
        for index in range(3):
            weight_copy(index, part).start()

    barrier = pltpu.get_barrier_semaphore()

    def greet(step, carry):
        pl.semaphore_signal(barrier, inc=1, device_id=peer(step), device_id_type=MESH)
        return carry

    lax.fori_loop(1, line, greet, 0)
    for device in (beside, sibling, across):
        pl.semaphore_signal(barrier, inc=1, device_id=device, device_id_type=MESH)
    pl.semaphore_wait(barrier, line + 2)

    for part in parts:
        cols = gather_cols[part]

        def spread(step, carry):
            for index, source in enumerate(inputs):
                pltpu.make_async_remote_copy(
                    src_ref=source.at[:, cols],
                    dst_ref=rows.at[index, slot(place), cols],
                    send_sem=send_sem.at[index, step],
                    recv_sem=recv_sem.at[index, part],
                    device_id=peer(step),
                    device_id_type=MESH,
                ).start()
            return carry

        lax.fori_loop(1, line, spread, 0)

    def side_copy(index, part):
        cols = gather_cols[part]
        return remote(
            rows.at[index, pl.ds(0, quarter), cols],
            rows.at[index, pl.ds(quarter, quarter), cols],
            side_sems,
            (index, part),
            beside,
        )

    def pair_copy(index, part):
        cols = gather_cols[part]
        return remote(
            rows.at[index, pl.ds(0, half), cols],
            rows.at[index, pl.ds(half, half), cols],
            pair_sems,
            (index, part),
            sibling,
        )

    def to_side(part):
        if part < len(gather_cols):
            for index in range(2):
                drain(rows.at[index, pl.ds(0, quarter), gather_cols[part]], recv_sem.at[index, part])
                side_copy(index, part).start()

    def to_pair(part):
        if part < len(gather_cols):
            for index in range(2):
                side_copy(index, part).wait_recv()
                pair_copy(index, part).start()

    other_half = columns(1 - tok, half_width)
    own_half = columns(tok, half_width)
    far_copy = [
        remote(
            rows.at[index, pl.ds(0, half), other_half], far_rows.at[index], far_sems, (index,), across
        )
        for index in range(2)
    ]
    far_keep = [
        pltpu.make_async_copy(
            far_rows.at[index], rows_out.at[index, pl.ds(group, half)], far_sems.at[2, index]
        )
        for index in range(2)
    ]
    far_relay = [
        pltpu.make_async_remote_copy(
            src_ref=far_rows.at[index],
            dst_ref=rows_out.at[index, pl.ds(group + half, half)],
            send_sem=far_sems.at[3, index],
            recv_sem=far_sems.at[4, index],
            device_id=sibling,
            device_id_type=MESH,
        )
        for index in range(2)
    ]
    near_keep = [
        pltpu.make_async_copy(
            rows.at[index, :, own_half], rows_out.at[index, pl.ds(0, group)], far_sems.at[5, index]
        )
        for index in range(2)
    ]

    to_side(0)
    to_side(1)
    to_pair(0)
    to_side(2)
    to_pair(1)
    for part in parts:
        cols = gather_cols[part]
        last = part == len(gather_cols) - 1
        for index in range(3):
            source = index // 2
            if index != 1:
                pair_copy(source, part).wait_recv()
            if last and index == 0:
                for copy in far_copy:
                    copy.start()
            if last and index == 2:
                for copy in near_keep:
                    copy.start()
            weight_copy(index, part).wait()
            term = right_product(rows[source, :, cols], weights[index, :, cols])
            if part == 0:
                values[index] = term
            else:
                values[index] += term
            if index == 0:
                to_side(part + 3)
            if index == 1:
                to_pair(part + 2)

    gate_value = values[0]
    up_value = values[1]
    hidden_grad = values[2]
    gate_sigmoid = jax.nn.sigmoid(gate_value)
    swish_gate = gate_value * gate_sigmoid
    hidden[0] = (
        hidden_grad * up_value * gate_sigmoid * (1.0 + gate_value * (1.0 - gate_sigmoid))
    ).astype(jnp.bfloat16)
    hidden[1] = (hidden_grad * swish_gate).astype(jnp.bfloat16)
    hidden[2] = (swish_gate * up_value).astype(jnp.bfloat16)
    hidden_local = [
        pltpu.make_async_copy(
            hidden.at[index], hidden_out.at[index, pl.ds(0, group)], hidden_sems.at[2, index]
        )
        for index in range(3)
    ]
    hidden_remote = [
        remote(
            hidden.at[index],
            hidden_out.at[index, pl.ds(group, group)],
            hidden_sems,
            (index,),
            across,
        )
        for index in range(3)
    ]
    for copy in hidden_local + hidden_remote:
        copy.start()

    def term_pair(index, part):
        cols = reduce_cols[part]
        return remote(
            pair_send.at[index, :, cols],
            pair_recv.at[index, :, cols],
            term_pair_sems,
            (index, part),
            sibling,
        )

    def term_side(index, part):
        cols = reduce_cols[part]
        return remote(
            side_send.at[index, :, cols],
            side_recv.at[index, :, cols],
            term_side_sems,
            (index, part),
            beside,
        )

    def product(index, cols):
        return jnp.dot(hidden[index], weights[index, :, cols], preferred_element_type=jnp.float32)

    def produce(index, part):
        cols = reduce_cols[part]
        if index == 0:
            term = product(2, cols)
        else:
            term = product(0, cols) + product(1, cols)
        own_term[index, :, cols] = term[:half]
        pair_send[index, :, cols] = term[half:].astype(jnp.bfloat16)
        term_pair(index, part).start()

    def fold_pair(index, part):
        cols = reduce_cols[part]
        term_pair(index, part).wait_recv()
        term = own_term[index, :, cols] + pair_recv[index, :, cols].astype(jnp.float32)
        own_term[index, :quarter, cols] = term[:quarter]
        side_send[index, :, cols] = term[quarter:].astype(jnp.bfloat16)
        term_side(index, part).start()

    def fold_side(index, part):
        cols = reduce_cols[part]
        term_side(index, part).wait_recv()
        line_send[index, :, cols] = (
            own_term[index, :quarter, cols] + side_recv[index, :, cols].astype(jnp.float32)
        ).astype(jnp.bfloat16)
        pltpu.make_async_copy(
            line_send.at[index, slot(place), cols],
            sums_out.at[index, slot(place), cols],
            sum_recv_sem.at[index],
        ).start()

        def hand(step, carry):
            pltpu.make_async_remote_copy(
                src_ref=line_send.at[index, slot((place + step) % line), cols],
                dst_ref=sums_out.at[index, slot(place), cols],
                send_sem=sum_send_sem.at[index, step],
                recv_sem=sum_recv_sem.at[index],
                device_id=peer(step),
                device_id_type=MESH,
            ).start()
            return carry

        lax.fori_loop(1, line, hand, 0)

    units = [(index, part) for part in range(len(reduce_cols)) for index in (1, 0)]
    for step in range(len(units) + FOLD_SIDE_LAG):
        if step < len(units):
            produce(*units[step])
        if step == 0:
            for index in range(2):
                far_copy[index].wait_recv()
                far_keep[index].start()
                far_relay[index].start()
        if 0 <= step - FOLD_PAIR_LAG < len(units):
            fold_pair(*units[step - FOLD_PAIR_LAG])
        if 0 <= step - FOLD_SIDE_LAG < len(units):
            fold_side(*units[step - FOLD_SIDE_LAG])

    for index in range(2):

        def sent(step, carry):
            drain(inputs[index], send_sem.at[index, step])
            drain(inputs[index], sum_send_sem.at[index, step])
            return carry

        lax.fori_loop(1, line, sent, 0)
        for part in parts:
            side_copy(index, part).wait_send()
            pair_copy(index, part).wait_send()
        for part in range(len(reduce_cols)):
            term_pair(index, part).wait_send()
            term_side(index, part).wait_send()
        far_copy[index].wait_send()
    for copy in far_keep + far_relay + near_keep + hidden_local + hidden_remote:
        copy.wait()
    for index in range(2):
        drain(sums_out.at[index], sum_recv_sem.at[index])


def block(tokens, upstream, gate_weight, up_weight, down_weight):
    own_rows, width = tokens.shape
    units = gate_weight.shape[0]
    count = lax.axis_size("blk")
    assert count % 4 == 0 and lax.axis_size("tok") == 2
    line = count // 4
    quarter = line * own_rows
    half = 2 * quarter
    group = 2 * half
    gathers, reduces = len(GATHER_PARTS), len(REDUCE_PARTS)
    bf16, f32 = jnp.bfloat16, jnp.float32
    hbm = pl.BlockSpec(memory_space=pl.ANY)
    dma = pltpu.SemaphoreType.DMA
    return pl.pallas_call(
        block_kernel,
        out_shape=(
            jax.ShapeDtypeStruct((2, 2 * group, width // 2), bf16),
            jax.ShapeDtypeStruct((3, 2 * group, units), bf16),
            jax.ShapeDtypeStruct((2, quarter, width), bf16),
        ),
        in_specs=[hbm] * 5,
        out_specs=(hbm, hbm, hbm),
        scratch_shapes=[
            pltpu.VMEM((3, units, width), bf16),
            pltpu.VMEM((2, group, width), bf16),
            pltpu.VMEM((3, group, units), f32),
            pltpu.VMEM((3, group, units), bf16),
            pltpu.VMEM((2, half, width // 2), bf16),
            pltpu.VMEM((2, half, width), f32),
            pltpu.VMEM((2, half, width), bf16),
            pltpu.VMEM((2, half, width), bf16),
            pltpu.VMEM((2, quarter, width), bf16),
            pltpu.VMEM((2, quarter, width), bf16),
            pltpu.VMEM((2, quarter, width), bf16),
            dma((3, gathers)),
            dma((2, line)),
            dma((2, gathers)),
            dma((2, 2, gathers)),
            dma((2, 2, gathers)),
            dma((6, 2)),
            dma((3, 3)),
            dma((2, 2, reduces)),
            dma((2, 2, reduces)),
            dma((2, line)),
            dma((2,)),
        ],
        compiler_params=pltpu.CompilerParams(
            collective_id=0, has_side_effects=True, vmem_limit_bytes=VMEM_LIMIT
        ),
    )(tokens, upstream, gate_weight, up_weight, down_weight)


def grad_kernel(
    rows_hbm,
    hidden_hbm,
    sums_hbm,
    mixed,
    input_grad,
    gate_grad,
    up_grad,
    down_grad,
    rows,
    hidden,
    sums,
    tiles,
    load_sems,
    sems,
):
    loads = [
        pltpu.make_async_copy(rows_hbm.at[0], rows.at[0], load_sems.at[0]),
        pltpu.make_async_copy(hidden_hbm.at[0], hidden.at[0], load_sems.at[1]),
        pltpu.make_async_copy(hidden_hbm.at[1], hidden.at[1], load_sems.at[2]),
        pltpu.make_async_copy(rows_hbm.at[1], rows.at[1], load_sems.at[3]),
        pltpu.make_async_copy(hidden_hbm.at[2], hidden.at[2], load_sems.at[4]),
        pltpu.make_async_copy(sums_hbm, sums, load_sems.at[5]),
    ]
    for copy in loads:
        copy.start()
    width = rows.shape[2] // GRAD_CHUNKS
    pending = [None] * GRAD_SLOTS
    step = 0
    for index, result in enumerate((gate_grad, up_grad, down_grad)):
        for copy in (loads[:2], loads[2:3], loads[3:5])[index]:
            copy.wait()
        for part in range(GRAD_CHUNKS):
            cols = pl.ds(part * width, width)
            where = step % GRAD_SLOTS
            if pending[where] is not None:
                pending[where].wait()
            tiles[where] = lax.dot_general(
                hidden[index],
                rows[index // 2, :, cols],
                (((0,), (0,)), ((), ())),
                preferred_element_type=jnp.float32,
            ).astype(jnp.bfloat16)
            pending[where] = pltpu.make_async_copy(
                tiles.at[where], result.at[:, cols], sems.at[where]
            )
            pending[where].start()
            step += 1
    own_rows, quarter = mixed.shape[0], sums.shape[1]
    pick = (
        lax.broadcasted_iota(jnp.int32, (own_rows, quarter), 1) % own_rows
        == lax.broadcasted_iota(jnp.int32, (own_rows, quarter), 0)
    ).astype(jnp.bfloat16)
    loads[5].wait()
    for index, result in enumerate((mixed, input_grad)):
        result[...] = jnp.dot(pick, sums[index], preferred_element_type=jnp.float32).astype(
            jnp.bfloat16
        )
    for copy in pending:
        if copy is not None:
            copy.wait()


def finish(rows, hidden, sums, own_rows):
    units = hidden.shape[2]
    width = rows.shape[2]
    hbm = pl.BlockSpec(memory_space=pl.ANY)
    vmem = pl.BlockSpec(memory_space=pltpu.VMEM)
    small = jax.ShapeDtypeStruct((own_rows, sums.shape[2]), jnp.bfloat16)
    shape = jax.ShapeDtypeStruct((units, width), jnp.bfloat16)
    return pl.pallas_call(
        grad_kernel,
        out_shape=(small, small, shape, shape, shape),
        in_specs=[hbm, hbm, hbm],
        out_specs=(vmem, vmem, hbm, hbm, hbm),
        scratch_shapes=[
            pltpu.VMEM(rows.shape, jnp.bfloat16),
            pltpu.VMEM(hidden.shape, jnp.bfloat16),
            pltpu.VMEM(sums.shape, jnp.bfloat16),
            pltpu.VMEM((GRAD_SLOTS, units, width // GRAD_CHUNKS), jnp.bfloat16),
            pltpu.SemaphoreType.DMA((6,)),
            pltpu.SemaphoreType.DMA((GRAD_SLOTS,)),
        ],
        compiler_params=pltpu.CompilerParams(vmem_limit_bytes=VMEM_LIMIT),
    )(rows, hidden, sums)


def local(tokens, *rest):
    rows, hidden, sums = block(tokens, *rest)
    return finish(rows, hidden, sums, tokens.shape[0])


def solution(mesh):
    return jax.shard_map(
        local,
        mesh=mesh,
        in_specs=(
            P(("blk", "tok"), None),
            P(("blk", "tok"), None),
            P("blk", None),
            P("blk", None),
            P("blk", None),
        ),
        out_specs=(
            P(("blk", "tok"), None),
            P(("blk", "tok"), None),
            P("blk", "tok"),
            P("blk", "tok"),
            P("blk", "tok"),
        ),
        check_vma=False,
    )
```

time: 63.7 us -> 64.5 us (1.013)
  Pallas kernels: 60 us -> 63.5 us
  local copies, waits for them, and re-layouts: 2.79 us -> 0 us
    pallas_call x2, Pallas kernels: 60 us -> 63.5 us  [the longest x1 52.7 us: block(): pl.pallas_call(block_kernel, out_shape=(jax.ShapeDtypeStruct((2, 2 * grou...]
    unnamed x2 -> x0, local copies, waits for them, and re-layouts: 2.79 us -> none
where the time goes in v2:
time: 64.5 us; the launch traced here: 64.3 us
  Pallas kernels  63.5 us (98%)
  between operations  0.8 us (1%)
    pallas_call x1, Pallas kernels, block(): pl.pallas_call(block_kernel, out_shape=(jax.ShapeDtypeStruct((2, 2 * grou...  52.7 us
    pallas_call x1, Pallas kernels, finish(): pl.pallas_call(grad_kernel, out_shape=(small, small, shape, shape, shape)...  10.8 us

profile of v2, /device:TPU:0, one launch (start us, length us, event | category | flops | bytes accessed | tf_op | source)
XLA Modules:
  0.0 64.3 jit_solution(14173376567493303139)
XLA Ops:
  0.6 52.7 %shard_map.92 = (bf16[2,64,4096]{2,1,0:T(8,128)(2,1)}, bf16[3,64,896]{2,1,0:T(8,128)(2,1)}, bf16[2,8,8192]{2,1,0:T(8,128)(2,1)}) custom-call(bf16[2,8192]{1,0:T(2,128)(2,1)} %tokens.1, bf16[2,8192]{1,0:T(2,128)(2,1)} %upstream.1, bf16[896,8192]{1,0:T(8,128)(2,1)} %gate_hbm.1, bf16[896,8192]{1,0:T(8,128)(2,1)} %up_hbm.1, bf16[896,8192]{1,0:T(8,128)(2,1)} %down_hbm.1), custom_call_target="tpu_custom_call" | custom-call | tf_op jit(solution)/shard_map/pallas_call | solution.py:388
  53.3 10.8 %shard_map.93 = (bf16[2,8192]{1,0:T(2,128)(2,1)}, bf16[2,8192]{1,0:T(2,128)(2,1)}, bf16[896,4096]{1,0:T(8,128)(2,1)}, bf16[896,4096]{1,0:T(8,128)(2,1)}, bf16[896,4096]{1,0:T(8,128)(2,1)}) custom-call(bf16[2,64,4096]{2,1,0:T(8,128)(2,1)} %get-tuple-element.8.rows_hbm, bf16[3,64,896]{2,1,0:T(8,128)(2,1)} %get-tuple-element.9.hidden_hbm, ...), custom_call_target="tpu_custom_call" | custom-call | tf_op jit(solution)/shard_map/pallas_call | solution.py:497

commit v3 on v2

v3 whole, which is shorter than its diff:
```python
import functools

import jax
import jax.numpy as jnp
from jax import lax
from jax.experimental import pallas as pl
from jax.experimental.pallas import tpu as pltpu
from jax.sharding import PartitionSpec as P

MESH = pl.DeviceIdType.MESH
VMEM_LIMIT = 63 * 1024 * 1024
GATHER_PARTS = (2, 3, 3)
REDUCE_PARTS = (4, 2, 2)
FOLD_PAIR_LAG = 1
FOLD_SIDE_LAG = 2
UNROLLED_LINE = 8
GRAD_CHUNKS = 4
GRAD_SLOTS = 3


def drain(ref, sem):
    pltpu.make_async_copy(ref, ref, sem).wait()


def columns(index, width):
    return pl.ds(pl.multiple_of(index * width, width), width)


def pieces(width, shares):
    unit = width // sum(shares)
    starts = [sum(shares[:index]) for index in range(len(shares))]
    return [pl.ds(start * unit, share * unit) for start, share in zip(starts, shares)]


def right_product(left, right):
    return lax.dot_general(
        left, right, (((1,), (1,)), ((), ())), preferred_element_type=jnp.float32
    )


def block_kernel(
    tokens,
    upstream,
    gate_hbm,
    up_hbm,
    down_hbm,
    rows_out,
    hidden_out,
    sums_out,
    weights,
    rows,
    values,
    hidden,
    far_rows,
    own_term,
    pair_send,
    pair_recv,
    side_send,
    side_recv,
    line_send,
    weight_sem,
    own_sem,
    send_sem,
    recv_sem,
    side_sems,
    pair_sems,
    far_sems,
    hidden_sems,
    term_pair_sems,
    term_side_sems,
    sum_send_sem,
    sum_recv_sem,
):
    line = lax.axis_size("blk") // 4
    me = lax.axis_index("blk")
    tok = lax.axis_index("tok")
    core = me % 2
    side = me // 2 % 2
    place = me // 4
    sibling = (me + 1 - 2 * core, tok)
    beside = (me + 2 - 4 * side, tok)
    across = (me, 1 - tok)
    own_rows, width = tokens.shape
    quarter = line * own_rows
    half = 2 * quarter
    group = 2 * half
    half_width = width // 2
    gather_cols = pieces(width, GATHER_PARTS)
    reduce_cols = pieces(width, REDUCE_PARTS)
    parts = range(len(gather_cols))
    sources = (gate_hbm, up_hbm, down_hbm)

    def peer(step):
        return ((place + step) % line * 4 + side * 2 + core, tok)

    def slot(index):
        return pl.ds(index * own_rows, own_rows)

    def each_step(body):
        if line <= UNROLLED_LINE:
            for step in range(1, line):
                body(step)
        else:

            def turn(step, carry):
                body(step)
                return carry

            lax.fori_loop(1, line, turn, 0)

    def remote(source, target, sems, where, device):
        return pltpu.make_async_remote_copy(
            src_ref=source,
            dst_ref=target,
            send_sem=sems.at[(0, *where)],
            recv_sem=sems.at[(1, *where)],
            device_id=device,
            device_id_type=MESH,
        )

    def weight_copy(index, part):
        cols = gather_cols[part]
        return pltpu.make_async_copy(
            sources[index].at[:, cols], weights.at[index, :, cols], weight_sem.at[index, part]
        )

    own_copies = [
        pltpu.make_async_copy(source, rows.at[index, slot(place)], own_sem.at[index])
        for index, source in enumerate((tokens, upstream))
    ]
    for copy in own_copies:
        copy.start()
    barrier = pltpu.get_barrier_semaphore()

    def greet(step):
        pl.semaphore_signal(barrier, inc=1, device_id=peer(step), device_id_type=MESH)

    each_step(greet)
    for device in (beside, sibling, across):
        pl.semaphore_signal(barrier, inc=1, device_id=device, device_id_type=MESH)
    for part in parts:
        for index in range(3):
            weight_copy(index, part).start()
    for copy in own_copies:
        copy.wait()
    pl.semaphore_wait(barrier, line + 2)

    for part in parts:
        cols = gather_cols[part]

        def spread(step):
            pltpu.make_async_remote_copy(
                src_ref=rows.at[:, slot(place), cols],
                dst_ref=rows.at[:, slot(place), cols],
                send_sem=send_sem.at[step],
                recv_sem=recv_sem.at[part, step],
                device_id=peer(step),
                device_id_type=MESH,
            ).start()

        each_step(spread)

    def side_copy(part):
        cols = gather_cols[part]
        return remote(
            rows.at[:, pl.ds(0, quarter), cols],
            rows.at[:, pl.ds(quarter, quarter), cols],
            side_sems,
            (part,),
            beside,
        )

    def pair_copy(part):
        cols = gather_cols[part]
        return remote(
            rows.at[:, pl.ds(0, half), cols],
            rows.at[:, pl.ds(half, half), cols],
            pair_sems,
            (part,),
            sibling,
        )

    def to_side(part):
        if part < len(gather_cols):
            cols = gather_cols[part]
            each_step(lambda step: drain(rows.at[:, slot(place), cols], recv_sem.at[part, step]))
            side_copy(part).start()

    def to_pair(part):
        if part < len(gather_cols):
            side_copy(part).wait_recv()
            pair_copy(part).start()

    other_half = columns(1 - tok, half_width)
    own_half = columns(tok, half_width)
    far_copy = remote(rows.at[:, pl.ds(0, half), other_half], far_rows, far_sems, (), across)
    far_keep = pltpu.make_async_copy(far_rows, rows_out.at[:, pl.ds(group, half)], far_sems.at[2])
    far_relay = pltpu.make_async_remote_copy(
        src_ref=far_rows,
        dst_ref=rows_out.at[:, pl.ds(group + half, half)],
        send_sem=far_sems.at[3],
        recv_sem=far_sems.at[4],
        device_id=sibling,
        device_id_type=MESH,
    )
    near_keep = pltpu.make_async_copy(
        rows.at[:, :, own_half], rows_out.at[:, pl.ds(0, group)], far_sems.at[5]
    )

    to_side(0)
    to_side(1)
    to_pair(0)
    for part in parts:
        cols = gather_cols[part]
        last = part == len(gather_cols) - 1
        pair_copy(part).wait_recv()
        if last:
            far_copy.start()
            near_keep.start()
        for index in range(3):
            weight_copy(index, part).wait()
            term = right_product(rows[index // 2, :, cols], weights[index, :, cols])
            if part == 0:
                values[index] = term
            else:
                values[index] += term
            if index == 0:
                to_pair(part + 1)
            if index == 1:
                to_side(part + 2)

    gate_value = values[0]
    up_value = values[1]
    hidden_grad = values[2]
    gate_sigmoid = jax.nn.sigmoid(gate_value)
    swish_gate = gate_value * gate_sigmoid
    hidden[0] = (
        hidden_grad * up_value * gate_sigmoid * (1.0 + gate_value * (1.0 - gate_sigmoid))
    ).astype(jnp.bfloat16)
    hidden[1] = (hidden_grad * swish_gate).astype(jnp.bfloat16)
    hidden[2] = (swish_gate * up_value).astype(jnp.bfloat16)
    hidden_local = pltpu.make_async_copy(
        hidden, hidden_out.at[:, pl.ds(0, group)], hidden_sems.at[2]
    )
    hidden_remote = remote(
        hidden, hidden_out.at[:, pl.ds(group, group)], hidden_sems, (), across
    )
    hidden_local.start()
    hidden_remote.start()

    def term_pair(part):
        cols = reduce_cols[part]
        return remote(
            pair_send.at[:, :, cols], pair_recv.at[:, :, cols], term_pair_sems, (part,), sibling
        )

    def term_side(part):
        cols = reduce_cols[part]
        return remote(
            side_send.at[:, :, cols], side_recv.at[:, :, cols], term_side_sems, (part,), beside
        )

    def product(index, cols):
        return jnp.dot(hidden[index], weights[index, :, cols], preferred_element_type=jnp.float32)

    def produce(part):
        cols = reduce_cols[part]
        for index in range(2):
            if index == 0:
                term = product(2, cols)
            else:
                term = product(0, cols) + product(1, cols)
            own_term[index, :, cols] = term[:half]
            pair_send[index, :, cols] = term[half:].astype(jnp.bfloat16)
        term_pair(part).start()

    def fold_pair(part):
        cols = reduce_cols[part]
        term_pair(part).wait_recv()
        for index in range(2):
            term = own_term[index, :, cols] + pair_recv[index, :, cols].astype(jnp.float32)
            own_term[index, :quarter, cols] = term[:quarter]
            side_send[index, :, cols] = term[quarter:].astype(jnp.bfloat16)
        term_side(part).start()

    def fold_side(part):
        cols = reduce_cols[part]
        term_side(part).wait_recv()
        for index in range(2):
            line_send[index, :, cols] = (
                own_term[index, :quarter, cols] + side_recv[index, :, cols].astype(jnp.float32)
            ).astype(jnp.bfloat16)

        def hand(step):
            pltpu.make_async_remote_copy(
                src_ref=line_send.at[:, slot((place + step) % line), cols],
                dst_ref=sums_out.at[:, slot(place), cols],
                send_sem=sum_send_sem.at[step],
                recv_sem=sum_recv_sem,
                device_id=peer(step),
                device_id_type=MESH,
            ).start()

        each_step(hand)
        pltpu.make_async_copy(
            line_send.at[:, slot(place), cols], sums_out.at[:, slot(place), cols], sum_recv_sem
        ).start()

    units = len(reduce_cols)
    for step in range(units + FOLD_SIDE_LAG):
        if step < units:
            produce(step)
        if step == 0:
            far_copy.wait_recv()
            far_keep.start()
            far_relay.start()
        if 0 <= step - FOLD_PAIR_LAG < units:
            fold_pair(step - FOLD_PAIR_LAG)
        if 0 <= step - FOLD_SIDE_LAG < units:
            fold_side(step - FOLD_SIDE_LAG)

    def sent(step):
        drain(rows.at[:, slot(place)], send_sem.at[step])
        drain(rows.at[:, slot(place)], sum_send_sem.at[step])

    each_step(sent)
    for part in parts:
        side_copy(part).wait_send()
        pair_copy(part).wait_send()
    for part in range(units):
        term_pair(part).wait_send()
        term_side(part).wait_send()
    far_copy.wait_send()
    for copy in (far_keep, far_relay, near_keep, hidden_local, hidden_remote):
        copy.wait()
    drain(sums_out, sum_recv_sem)


def block(tokens, upstream, gate_weight, up_weight, down_weight):
    own_rows, width = tokens.shape
    units = gate_weight.shape[0]
    count = lax.axis_size("blk")
    assert count % 4 == 0 and lax.axis_size("tok") == 2
    line = count // 4
    quarter = line * own_rows
    half = 2 * quarter
    group = 2 * half
    gathers, reduces = len(GATHER_PARTS), len(REDUCE_PARTS)
    bf16, f32 = jnp.bfloat16, jnp.float32
    hbm = pl.BlockSpec(memory_space=pl.ANY)
    dma = pltpu.SemaphoreType.DMA
    return pl.pallas_call(
        block_kernel,
        out_shape=(
            jax.ShapeDtypeStruct((2, 2 * group, width // 2), bf16),
            jax.ShapeDtypeStruct((3, 2 * group, units), bf16),
            jax.ShapeDtypeStruct((2, quarter, width), bf16),
        ),
        in_specs=[hbm] * 5,
        out_specs=(hbm, hbm, hbm),
        scratch_shapes=[
            pltpu.VMEM((3, units, width), bf16),
            pltpu.VMEM((2, group, width), bf16),
            pltpu.VMEM((3, group, units), f32),
            pltpu.VMEM((3, group, units), bf16),
            pltpu.VMEM((2, half, width // 2), bf16),
            pltpu.VMEM((2, half, width), f32),
            pltpu.VMEM((2, half, width), bf16),
            pltpu.VMEM((2, half, width), bf16),
            pltpu.VMEM((2, quarter, width), bf16),
            pltpu.VMEM((2, quarter, width), bf16),
            pltpu.VMEM((2, quarter, width), bf16),
            dma((3, gathers)),
            dma((2,)),
            dma((line,)),
            dma((gathers, line)),
            dma((2, gathers)),
            dma((2, gathers)),
            dma((6,)),
            dma((3,)),
            dma((2, reduces)),
            dma((2, reduces)),
            dma((line,)),
            dma(()),
        ],
        compiler_params=pltpu.CompilerParams(
            collective_id=0, has_side_effects=True, vmem_limit_bytes=VMEM_LIMIT
        ),
    )(tokens, upstream, gate_weight, up_weight, down_weight)


def grad_kernel(
    rows_hbm,
    hidden_hbm,
    sums_hbm,
    mixed,
    input_grad,
    gate_grad,
    up_grad,
    down_grad,
    rows,
    hidden,
    sums,
    tiles,
    load_sems,
    sems,
):
    loads = [
        pltpu.make_async_copy(rows_hbm.at[0], rows.at[0], load_sems.at[0]),
        pltpu.make_async_copy(hidden_hbm.at[0], hidden.at[0], load_sems.at[1]),
        pltpu.make_async_copy(hidden_hbm.at[1], hidden.at[1], load_sems.at[2]),
        pltpu.make_async_copy(rows_hbm.at[1], rows.at[1], load_sems.at[3]),
        pltpu.make_async_copy(hidden_hbm.at[2], hidden.at[2], load_sems.at[4]),
        pltpu.make_async_copy(sums_hbm, sums, load_sems.at[5]),
    ]
    for copy in loads:
        copy.start()
    width = rows.shape[2] // GRAD_CHUNKS
    pending = [None] * GRAD_SLOTS
    step = 0
    for index, result in enumerate((gate_grad, up_grad, down_grad)):
        for copy in (loads[:2], loads[2:3], loads[3:5])[index]:
            copy.wait()
        for part in range(GRAD_CHUNKS):
            cols = pl.ds(part * width, width)
            where = step % GRAD_SLOTS
            if pending[where] is not None:
                pending[where].wait()
            tiles[where] = lax.dot_general(
                hidden[index],
                rows[index // 2, :, cols],
                (((0,), (0,)), ((), ())),
                preferred_element_type=jnp.float32,
            ).astype(jnp.bfloat16)
            pending[where] = pltpu.make_async_copy(
                tiles.at[where], result.at[:, cols], sems.at[where]
            )
            pending[where].start()
            step += 1
    own_rows, quarter = mixed.shape[0], sums.shape[1]
    pick = (
        lax.broadcasted_iota(jnp.int32, (own_rows, quarter), 1) % own_rows
        == lax.broadcasted_iota(jnp.int32, (own_rows, quarter), 0)
    ).astype(jnp.bfloat16)
    loads[5].wait()
    for index, result in enumerate((mixed, input_grad)):
        result[...] = jnp.dot(pick, sums[index], preferred_element_type=jnp.float32).astype(
            jnp.bfloat16
        )
    for copy in pending:
        if copy is not None:
            copy.wait()


def finish(rows, hidden, sums, own_rows):
    units = hidden.shape[2]
    width = rows.shape[2]
    hbm = pl.BlockSpec(memory_space=pl.ANY)
    vmem = pl.BlockSpec(memory_space=pltpu.VMEM)
    small = jax.ShapeDtypeStruct((own_rows, sums.shape[2]), jnp.bfloat16)
    shape = jax.ShapeDtypeStruct((units, width), jnp.bfloat16)
    return pl.pallas_call(
        grad_kernel,
        out_shape=(small, small, shape, shape, shape),
        in_specs=[hbm, hbm, hbm],
        out_specs=(vmem, vmem, hbm, hbm, hbm),
        scratch_shapes=[
            pltpu.VMEM(rows.shape, jnp.bfloat16),
            pltpu.VMEM(hidden.shape, jnp.bfloat16),
            pltpu.VMEM(sums.shape, jnp.bfloat16),
            pltpu.VMEM((GRAD_SLOTS, units, width // GRAD_CHUNKS), jnp.bfloat16),
            pltpu.SemaphoreType.DMA((6,)),
            pltpu.SemaphoreType.DMA((GRAD_SLOTS,)),
        ],
        compiler_params=pltpu.CompilerParams(vmem_limit_bytes=VMEM_LIMIT),
    )(rows, hidden, sums)


def local(tokens, *rest):
    rows, hidden, sums = block(tokens, *rest)
    return finish(rows, hidden, sums, tokens.shape[0])


def solution(mesh):
    return jax.shard_map(
        local,
        mesh=mesh,
        in_specs=(
            P(("blk", "tok"), None),
            P(("blk", "tok"), None),
            P("blk", None),
            P("blk", None),
            P("blk", None),
        ),
        out_specs=(
            P(("blk", "tok"), None),
            P(("blk", "tok"), None),
            P("blk", "tok"),
            P("blk", "tok"),
            P("blk", "tok"),
        ),
        check_vma=False,
    )
```

time: 64.5 us -> 60.3 us (0.935)
  Pallas kernels: 63.5 us -> 59.4 us
    pallas_call x1, Pallas kernels: 52.7 us -> 48.5 us  [block(): pl.pallas_call(block_kernel, out_shape=(jax.ShapeDtypeStruct((2, 2 * grou...]
where the time goes in v3:
time: 60.3 us; the launch traced here: 60.2 us
  Pallas kernels  59.4 us (99%)
  between operations  0.8 us (1%)
    pallas_call x1, Pallas kernels, block(): pl.pallas_call(block_kernel, out_shape=(jax.ShapeDtypeStruct((2, 2 * grou...  48.5 us
    pallas_call x1, Pallas kernels, finish(): pl.pallas_call(grad_kernel, out_shape=(small, small, shape, shape, shape)...  10.8 us

profile of v3, /device:TPU:0, one launch (start us, length us, event | category | flops | bytes accessed | tf_op | source)
XLA Modules:
  0.0 60.2 jit_solution(15273167976333072839)
XLA Ops:
  0.6 48.5 %shard_map.92 = (bf16[2,64,4096]{2,1,0:T(8,128)(2,1)}, bf16[3,64,896]{2,1,0:T(8,128)(2,1)}, bf16[2,8,8192]{2,1,0:T(8,128)(2,1)}) custom-call(bf16[2,8192]{1,0:T(2,128)(2,1)} %tokens.1, bf16[2,8192]{1,0:T(2,128)(2,1)} %upstream.1, bf16[896,8192]{1,0:T(8,128)(2,1)} %gate_hbm.1, bf16[896,8192]{1,0:T(8,128)(2,1)} %up_hbm.1, bf16[896,8192]{1,0:T(8,128)(2,1)} %down_hbm.1), custom_call_target="tpu_custom_call" | custom-call | tf_op jit(solution)/shard_map/pallas_call | solution.py:352
  49.2 10.8 %shard_map.93 = (bf16[2,8192]{1,0:T(2,128)(2,1)}, bf16[2,8192]{1,0:T(2,128)(2,1)}, bf16[896,4096]{1,0:T(8,128)(2,1)}, bf16[896,4096]{1,0:T(8,128)(2,1)}, bf16[896,4096]{1,0:T(8,128)(2,1)}) custom-call(bf16[2,64,4096]{2,1,0:T(8,128)(2,1)} %get-tuple-element.8.rows_hbm, bf16[3,64,896]{2,1,0:T(8,128)(2,1)} %get-tuple-element.9.hidden_hbm, ...), custom_call_target="tpu_custom_call" | custom-call | tf_op jit(solution)/shard_map/pallas_call | solution.py:462
